TPU v7x, 32 devices: a whole 2x2x4 slice. The times are simulated.
32 devices in a mesh: row: 8 (over z, y), col: 4 (over x, core).
Axes of the slice: x: 2, y: 2, z: 4, core: 2. Of those that a mesh axis runs over, the one named last changes fastest.
Arguments:
- layer_input: bfloat16 [1024, 12288], P(None, 'row'), may hold values from -6 to 6
- hidden_pre: bfloat16 [1024, 24576], P(None, 'col'), may hold values from -6 to 6
- out_grad: bfloat16 [1024, 12288], P(None, 'row'), may hold values from -8 to 8
- w_up: bfloat16 [12288, 24576], P('row', 'col'), may hold values from -0.0546875 to 0.0546875
- w_down: bfloat16 [24576, 12288], P('col', 'row'), may hold values from -0.0390625 to 0.0390625
Outputs:
- in_grad: bfloat16 [1024, 12288], P('col', 'row')
- up_grad: bfloat16 [12288, 24576], P('row', 'col')
- down_grad: bfloat16 [24576, 12288], P('col', 'row')
All inputs are finite; a program needn't handle non-finite values.
Results may differ from a plain program's by a relative error of at most 0.0051.
Values may be sent and summed in bfloat16 or wider, within the bound.
A program may use at most 320 MiB of HBM per device.

v0:
```python
import math
import jax
import jax.numpy as jnp
from jax import lax
from jax.sharding import PartitionSpec as P

GELU_COEF = 0.7978845608
CUBIC_COEF = 0.044715
CONTRACT_LAST = (((1,), (1,)), ((), ()))
CONTRACT_FIRST = (((0,), (0,)), ((), ()))


def gelu_value(pre_act):
    inner = GELU_COEF * (pre_act + CUBIC_COEF * pre_act * pre_act * pre_act)
    return 0.5 * pre_act * (1.0 + jnp.tanh(inner))


def gelu_slope(pre_act):
    inner = GELU_COEF * (pre_act + CUBIC_COEF * pre_act * pre_act * pre_act)
    tangent = jnp.tanh(inner)
    return 0.5 * (1.0 + tangent) + 0.5 * pre_act * (1.0 - tangent * tangent) * GELU_COEF * (
        1.0 + 3.0 * CUBIC_COEF * pre_act * pre_act
    )


def body(layer_input, hidden_pre, out_grad, w_up, w_down):
    token_count = out_grad.shape[0]
    scaling = 1.0 / math.sqrt(token_count)
    pre_act = hidden_pre.astype(jnp.float32)
    activated = gelu_value(pre_act).astype(jnp.bfloat16)
    down_total = lax.dot_general(
        activated, out_grad, CONTRACT_FIRST, preferred_element_type=jnp.float32
    )
    down_grad = (down_total * scaling).astype(jnp.bfloat16)
    local_sum = lax.dot_general(out_grad, w_down, CONTRACT_LAST, preferred_element_type=jnp.float32)
    summed = lax.psum(local_sum, "row")
    hidden_grad = (summed * gelu_slope(pre_act)).astype(jnp.bfloat16)
    up_total = lax.dot_general(
        layer_input, hidden_grad, CONTRACT_FIRST, preferred_element_type=jnp.float32
    )
    in_partial = lax.dot_general(
        hidden_grad, w_up, CONTRACT_LAST, preferred_element_type=jnp.float32
    )
    up_grad = (up_total * scaling).astype(jnp.bfloat16)
    in_grad = lax.psum_scatter(in_partial, "col", scatter_dimension=0, tiled=True).astype(
        jnp.bfloat16
    )
    return (in_grad, up_grad, down_grad)


def solution(mesh):
    placed = (P(None, "row"), P(None, "col"), P(None, "row"), P("row", "col"), P("col", "row"))
    return jax.shard_map(
        body,
        mesh=mesh,
        in_specs=placed,
        out_specs=(P("col", "row"), P("row", "col"), P("col", "row")),
        check_vma=False,
    )
```

profile of v0, /device:TPU:0, one launch (start us, length us, event | category | flops | bytes accessed | tf_op | source)
XLA Modules:
  0.0 922.6 jit_solution(7426446463446432995)
XLA Ops:
  7.2 0.0 copy-start
  7.2 0.0 all-reduce.2.cloned.1.call-start
  7.2 1.8 copy-done
  9.1 25.3 %fusion.21 = f32[1024,6144]{1,0:T(8,128)} fusion(bf16[1024,1536]{1,0:T(8,128)(2,1)S(1)} %copy-done, bf16[6144,1536]{1,0:T(8,128)(2,1)} %param.9), kind=kOutput, calls=%fused_computation.29 | convolution fusion | flops 19327352832 | bytes 47185920 | tf_op jit(solution)/shard_map/dot_general | solution.py:35
  34.4 0.0 all-reduce.2.cloned.1.call-update
  34.4 0.0 reduce-scatter.2.cloned.1.call-start
  34.5 745.5 %all-reduce.2.cloned.1.call-done = f32[1024,6144]{1,0:T(8,128)} async-done(((f32[1024,6144]{1,0:T(8,128)}), f32[1024,6144]{1,0:T(8,128)}) %all-reduce.2.cloned.1.call-update) | async-done | bytes 25165840 | tf_op jit(solution)/shard_map/psum | solution.py:36
  780.0 19.7 %fusion.6 = bf16[1024,6144]{1,0:T(8,128)(2,1)S(1)} fusion(f32[1024,6144]{1,0:T(8,128)} %all-reduce.2.cloned.1.call-done, bf16[1024,6144]{1,0:T(8,128)(2,1)} %param.6), kind=kLoop, calls=%fused_computation.15 | loop fusion | flops 125829120 | bytes 50331648 | tf_op jit(solution)/shard_map/convert_element_type | solution.py:37
  799.8 0.0 copy-start.1
  799.8 4.8 copy-done.1
  804.5 24.3 %fusion.22 = f32[1024,1536]{1,0:T(8,128)} fusion(bf16[1024,6144]{1,0:T(8,128)(2,1)S(1)} %fusion.6, bf16[1536,6144]{1,0:T(8,128)(2,1)} %param.8), kind=kOutput, calls=%fused_computation.30 | convolution fusion | flops 19327352832 | bytes 37748736 | tf_op jit(solution)/shard_map/dot_general | solution.py:41
  828.8 0.0 reduce-scatter.2.cloned.1.call-update
  828.9 0.0 copy-start.2
  828.9 31.3 %multiply_convert_fusion = bf16[6144,1536]{1,0:T(8,128)(2,1)} fusion(bf16[1024,1536]{1,0:T(8,128)(2,1)S(1)} %copy-done, bf16[1024,6144]{1,0:T(8,128)(2,1)} %param.6), kind=kOutput, calls=%fused_computation.7 | convolution fusion | flops 19409141760 | bytes 34603008 | tf_op jit(solution)/shard_map/dot_general | solution.py:31
  860.2 0.0 copy-done.2
  860.2 28.7 %fusion.11 = bf16[1536,6144]{0,1:T(8,128)(2,1)} fusion(bf16[1024,6144]{1,0:T(8,128)(2,1)} %copy-done.1, bf16[1024,1536]{1,0:T(8,128)(2,1)S(1)} %copy-done.2), kind=kOutput, calls=%fused_computation.20 | convolution fusion | flops 19346227200 | bytes 34603008 | tf_op jit(solution)/shard_map/dot_general | solution.py:38
  888.8 24.6 %copy.8 = bf16[1536,6144]{1,0:T(8,128)(2,1)} copy(bf16[1536,6144]{0,1:T(8,128)(2,1)} %fusion.11) | data formatting | bytes 37748736
  913.4 0.0 reduce-scatter.2.cloned.1.call-done
  913.4 2.4 convert_element_type.23
Async XLA Ops:
  7.2 1.9 copy-start
  7.2 772.8 %all-reduce.2.cloned.1.call-start = ((), (), s32[]{:S(2)}) async-start(), calls=%async_computation.1 | async-start | bytes 50331648 | tf_op jit(solution)/shard_map/psum | solution.py:36
  34.4 879.0 %reduce-scatter.2.cloned.1.call-start = ((), (), s32[]{:S(2)}) async-start(), calls=%async_computation.2 | async-start | bytes 7864320 | tf_op jit(solution)/shard_map/reduce_scatter | solution.py:45
  799.8 4.8 copy-start.1
  828.9 31.3 %copy-start.2 = (bf16[1024,1536]{1,0:T(8,128)(2,1)S(1)}, bf16[1024,1536]{1,0:T(8,128)(2,1)}, u32[]{:S(2)}) copy-start(bf16[1024,1536]{1,0:T(8,128)(2,1)} %param.5) | copy-start | bytes 9437188
Sparse Core Ops, SparseCore 0:
  34.6 745.4 all-reduce.1
  829.0 57.9 reduce-scatter.1
where the time goes:
time: 923 us
  waiting for transfers between devices  746 us (81%)
  matrix products  110 us (12%)
  local copies, waits for them, and re-layouts  31.2 us (3%)
  other arithmetic  22.1 us (2%)
  between operations  14.1 us (2%)
    psum x1, waiting for transfers between devices, body(): summed = lax.psum(local_sum, 'row')  746 us
    dot_general x1, matrix products, body(): lax.dot_general(activated, out_grad, CONTRACT_FIRST, preferred_element_ty...  31.3 us
    unnamed x7, local copies, waits for them, and re-layouts  31.2 us
    dot_general x1, matrix products, body(): lax.dot_general(layer_input, hidden_grad, CONTRACT_FIRST, preferred_eleme...  28.7 us
    dot_general x1, matrix products, body(): lax.dot_general(out_grad, w_down, CONTRACT_LAST, preferred_element_type=j...  25.3 us
    dot_general x1, matrix products, body(): lax.dot_general(hidden_grad, w_up, CONTRACT_LAST, preferred_element_type=...  24.3 us
    convert_element_type x1, other arithmetic, body(): hidden_grad = (summed * gelu_slope(pre_act)).astype(jnp.bfloat16)  19.7 us
  transfers between devices with their start and end apart: 2, of which 1 were waited for; matrix products, arithmetic and copies ran while one was open for 9% of the time, Pallas kernels for 0%

commit v1 on v0

--- a/solution.py
+++ b/solution.py
@@ -1,3 +1,4 @@
+import functools
 import math
 import jax
 import jax.numpy as jnp
@@ -8,6 +9,15 @@
 CUBIC_COEF = 0.044715
 CONTRACT_LAST = (((1,), (1,)), ((), ()))
 CONTRACT_FIRST = (((0,), (0,)), ((), ()))
+
+
+def draw_the_floor(x0, a_name):
+    left_arr = lax.all_gather(x0, axis_name=a_name)
+    formed = jnp.sum(left_arr, 0)
+    return formed
+
+
+run_keys = functools.partial(draw_the_floor, a_name="row")
 
 
 def gelu_value(pre_act):
@@ -33,7 +43,7 @@
     )
     down_grad = (down_total * scaling).astype(jnp.bfloat16)
     local_sum = lax.dot_general(out_grad, w_down, CONTRACT_LAST, preferred_element_type=jnp.float32)
-    summed = lax.psum(local_sum, "row")
+    summed = run_keys(local_sum)
     hidden_grad = (summed * gelu_slope(pre_act)).astype(jnp.bfloat16)
     up_total = lax.dot_general(
         layer_input, hidden_grad, CONTRACT_FIRST, preferred_element_type=jnp.float32

time: 923 us -> 4030 us (4.37)
  waiting for transfers between devices: 746 us -> 3790 us
  other arithmetic: 22.1 us -> 92.3 us
    all_gather x0 -> x1, waiting for transfers between devices: none -> 3790 us  [draw_the_floor(): left_arr = lax.all_gather(x0, axis_name=a_name)]
    psum x1 -> x0, waiting for transfers between devices: 746 us -> none  [body(): summed = lax.psum(local_sum, 'row')]
    reduce_sum x0 -> x1, other arithmetic: none -> 70.2 us  [draw_the_floor(): formed = jnp.sum(left_arr, 0)]
  transfers between devices with their start and end apart: 2 -> 2, of which waited for: 1 -> 1; matrix products, arithmetic and copies ran while one was open for 9% -> 2% of each run, Pallas kernels for 0% -> 0%
where the time goes in v1:
time: 4030 us
  waiting for transfers between devices  3790 us (94%)
  matrix products  110 us (3%)
  other arithmetic  92.3 us (2%)
    all_gather x1, waiting for transfers between devices, draw_the_floor(): left_arr = lax.all_gather(x0, axis_name=a_name)  3790 us
  transfers between devices with their start and end apart: 2, of which 1 were waited for; matrix products, arithmetic and copies ran while one was open for 2% of the time, Pallas kernels for 0%

profile of v1, /device:TPU:0, one launch (start us, length us, event | category | flops | bytes accessed | tf_op | source)
XLA Modules:
  0.0 4033.7 jit_solution(5011617372208687561)
XLA Ops:
  7.2 0.0 copy-start
  7.2 0.0 all-gather.3.cloned.1.call-start
  7.2 1.8 copy-done
  9.1 25.3 fusion.21
  34.4 0.0 all-gather.3.cloned.1.call-update
  34.4 0.2 reduce-scatter.2.cloned.1.call-start
  34.6 3786.2 %all-gather.3.cloned.1.call-done = f32[8192,6144]{1,0:T(8,128)} async-done(((f32[1024,6144]{1,0:T(8,128)}), f32[8192,6144]{1,0:T(8,128)}) %all-gather.3.cloned.1.call-update) | async-done | bytes 201326608 | tf_op jit(solution)/shard_map/all_gather | solution.py:15
  3820.8 70.2 %reduce_sum.9 = f32[1024,6144]{1,0:T(8,128)} reduce(f32[8,1024,6144]{2,1,0:T(8,128)} %bitcast, f32[]{:T(128)} %constant.7.clone.1), dimensions={0}, to_apply=%region_0.0 | reduce | flops 44040192 | bytes 226492416 | tf_op jit(solution)/shard_map/reduce_sum | solution.py:16
  3891.0 19.7 fusion.6
  3910.7 0.0 copy-start.1
  3910.8 4.8 copy-done.1
  3915.5 24.3 fusion.22
  3939.8 0.0 reduce-scatter.2.cloned.1.call-update
  3939.8 0.0 copy-start.2
  3939.8 31.4 multiply_convert_fusion
  3971.3 0.0 copy-done.2
  3971.3 28.7 fusion.11
  3999.9 24.6 copy.8
  4024.5 0.0 reduce-scatter.2.cloned.1.call-done
  4024.5 2.4 convert_element_type.23
Async XLA Ops:
  7.2 1.9 copy-start
  7.2 3813.7 %all-gather.3.cloned.1.call-start = ((), (), s32[]{:S(2)}) async-start(), calls=%async_computation.2 | async-start | bytes 226492416 | tf_op jit(solution)/shard_map/all_gather | solution.py:15
  34.4 3990.1 %reduce-scatter.2.cloned.1.call-start = ((), (), s32[]{:S(2)}) async-start(), calls=%async_computation.1 | async-start | bytes 7864320 | tf_op jit(solution)/shard_map/reduce_scatter | solution.py:55
  3910.7 4.8 copy-start.1
  3939.8 31.4 copy-start.2
Sparse Core Ops, SparseCore 0:
  34.5 3786.2 all-gather.2
  3939.9 58.8 reduce-scatter.1
